TPU v7x, 256 devices: a whole 4x4x8 slice. The times are simulated.
256 devices in a mesh: section: 32 (over x, z), expert: 8 (over y, core).
Axes of the slice: x: 4, y: 4, z: 8, core: 2. Of those that a mesh axis runs over, the one named last changes fastest.
Arguments:
- tokens: bfloat16 [2048, 4096], P('expert', 'section'), may hold values from -6 to 6
- routes: int32 [2048, 2], P('expert'), may hold values from 0 to 7, all different within a row; in each aligned block of 256 rows (0 to 255, 256 to 511, ...) at most 80 rows name the same one
- mix_weights: float32 [2048, 2], P('expert'), may hold values from 0.2 to 1
- w_gate: bfloat16 [8, 4096, 8192], P('expert', None, 'section'), may hold values from -0.1875 to 0.1875
- w_up: bfloat16 [8, 4096, 8192], P('expert', None, 'section'), may hold values from -0.1875 to 0.1875
- w_down: bfloat16 [8, 8192, 4096], P('expert', 'section'), may hold values from -0.125 to 0.125
- upstream: bfloat16 [2048, 4096], P('expert', 'section'), may hold values from -6 to 6
Outputs:
- mixed: bfloat16 [2048, 4096], P('expert', 'section')
- grad_tokens: bfloat16 [2048, 4096], P('expert', 'section')
- grad_mix: float32 [2048, 2], P('expert')
- grad_gate: bfloat16 [8, 4096, 8192], P('expert', None, 'section')
- grad_up: bfloat16 [8, 4096, 8192], P('expert', None, 'section')
- grad_down: bfloat16 [8, 8192, 4096], P('expert', 'section')
Inputs may be any that keep to these rules, and one draw needn't show every extreme that they name: `routes`: each token names 2 different experts. Among the 256 tokens of one index of the expert axis no expert is named more than 80 times, and in some such block one expert is named exactly 80 times.
All inputs are finite; a program needn't handle non-finite values.
Results may differ from a plain program's by a relative error of at most 0.02.
Values may be sent and summed in bfloat16 or wider, within the bound.
No kernel may reach another device: no remote copies, remote signals or barrier semaphores. Data moves between devices by JAX's collectives and lax.ppermute only.
A program may use at most 128 MiB of HBM per device.

v0:
```python
import jax
import jax.numpy as jnp
from jax import lax
from jax.sharding import PartitionSpec as P

highest = lax.Precision.HIGHEST


def slot_tables(route_rows, mix_rows, capacity, experts):
    tok_count, top_count = route_rows.shape
    flat_routes = route_rows.reshape(-1)
    onehot = (flat_routes[:, None] == jnp.arange(experts, dtype=jnp.int32)[None, :]).astype(
        jnp.int32
    )
    earlier = jnp.cumsum(onehot, axis=0) - onehot
    position = jnp.sum(earlier * onehot, axis=1)
    target = (flat_routes * capacity + position).reshape(tok_count, top_count)
    slot_ids = jnp.arange(experts * capacity, dtype=jnp.int32)
    hits = target[None, :, :] == slot_ids[:, None, None]
    matches = hits.astype(jnp.float32)
    select = jnp.sum(matches, axis=2)
    weighted = jnp.sum(matches * mix_rows[None, :, :], axis=2)
    token_ids = jnp.arange(tok_count, dtype=jnp.int32)
    slot_token = jnp.sum(jnp.sum(hits.astype(jnp.int32), axis=2) * token_ids[None, :], axis=1)
    return (target, select, weighted, slot_token)


def per_device(tokens, routes, mix_weights, w_gate, w_up, w_down, upstream):
    experts = lax.axis_size("expert")
    tok_count = tokens.shape[0]
    top_count = routes.shape[1]
    capacity = 5 * tok_count * top_count // (4 * experts)
    slot_total = experts * capacity
    target, select, weighted, slot_token = slot_tables(routes, mix_weights, capacity, experts)
    slot_fill = jnp.sum(select, axis=1)
    slot_scale = jnp.sum(weighted, axis=1)
    gate_local = w_gate[0]
    up_local = w_up[0]
    down_local = w_down[0]

    def collect(source, factor):
        taken = source[slot_token].astype(jnp.float32)
        return (taken * factor[:, None]).astype(jnp.bfloat16)

    def to_experts(source, factor):
        block = collect(source, factor)
        arrived = lax.all_to_all(
            block.reshape(experts, capacity, -1), "expert", split_axis=0, concat_axis=0, tiled=True
        )
        whole = lax.all_gather(arrived, "section", axis=2, tiled=True)
        return whole.reshape(slot_total, -1)

    def to_sources(partial_value):
        summed = lax.psum_scatter(
            partial_value.reshape(experts, capacity, -1).astype(jnp.bfloat16),
            "section",
            scatter_dimension=2,
            tiled=True,
        )
        back = lax.all_to_all(summed, "expert", split_axis=0, concat_axis=0, tiled=True)
        return back.reshape(slot_total, -1)

    dispatched = to_experts(tokens, slot_fill)
    act_gate = jnp.dot(dispatched, gate_local, preferred_element_type=jnp.float32)
    act_up = jnp.dot(dispatched, up_local, preferred_element_type=jnp.float32)
    sig = jax.nn.sigmoid(act_gate)
    silu_gate = act_gate * sig
    hidden = (silu_gate * act_up).astype(jnp.bfloat16)
    partial_value = jnp.dot(hidden, down_local, preferred_element_type=jnp.float32)
    returned = to_sources(partial_value).astype(jnp.float32)
    moe_out = jnp.dot(weighted.T, returned, precision=highest)
    mixed = (tokens.astype(jnp.float32) + moe_out).astype(jnp.bfloat16)
    picked = returned[target]
    upstream_wide = upstream.astype(jnp.float32)
    mix_terms = jnp.einsum("tkd,td->tk", picked, upstream_wide, precision=highest)
    grad_mix = lax.psum(mix_terms, "section")
    grad_rows = to_experts(upstream, slot_scale)
    grad_hidden = lax.dot_general(
        grad_rows, down_local, (((1,), (1,)), ((), ())), preferred_element_type=jnp.float32
    )
    grad_down = lax.dot_general(
        hidden, grad_rows, (((0,), (0,)), ((), ())), preferred_element_type=jnp.float32
    ).astype(jnp.bfloat16)
    dsilu = sig * (1.0 + act_gate * (1.0 - sig))
    grad_act_gate = (grad_hidden * act_up * dsilu).astype(jnp.bfloat16)
    grad_act_up = (grad_hidden * silu_gate).astype(jnp.bfloat16)
    grad_gate = lax.dot_general(
        dispatched, grad_act_gate, (((0,), (0,)), ((), ())), preferred_element_type=jnp.float32
    ).astype(jnp.bfloat16)
    grad_up = lax.dot_general(
        dispatched, grad_act_up, (((0,), (0,)), ((), ())), preferred_element_type=jnp.float32
    ).astype(jnp.bfloat16)
    first = lax.dot_general(
        grad_act_gate, gate_local, (((1,), (1,)), ((), ())), preferred_element_type=jnp.float32
    )
    second = lax.dot_general(
        grad_act_up, up_local, (((1,), (1,)), ((), ())), preferred_element_type=jnp.float32
    )
    back_rows = to_sources(first + second).astype(jnp.float32)
    grad_moe = jnp.dot(select.T, back_rows, precision=highest)
    grad_tokens = (upstream_wide + grad_moe).astype(jnp.bfloat16)
    return (mixed, grad_tokens, grad_mix, grad_gate[None], grad_up[None], grad_down[None])


def solution(mesh):
    return jax.shard_map(
        per_device,
        mesh=mesh,
        in_specs=(
            P("expert", "section"),
            P("expert", None),
            P("expert", None),
            P("expert", None, "section"),
            P("expert", None, "section"),
            P("expert", "section", None),
            P("expert", "section"),
        ),
        out_specs=(
            P("expert", "section"),
            P("expert", "section"),
            P("expert", None),
            P("expert", None, "section"),
            P("expert", None, "section"),
            P("expert", "section", None),
        ),
        check_vma=False,
    )
```

profile of v0, /device:TPU:8, one launch (start us, length us, event | category | flops | bytes accessed | tf_op | source)
XLA Modules:
  0.0 783.5 jit_solution(15971595313948356913)
XLA Ops:
  8.5 1.1 reduce-window.6
  11.4 2.1 select_reduce_fusion
  13.6 2.0 gather_fusion
  15.7 10.3 %all_to_all.20 = bf16[8,80,128]{2,1,0:T(8,128)(2,1)} all-to-all(bf16[8,80,128]{2,1,0:T(8,128)(2,1)S(1)} %fusion.17), channel_id=1, replica_groups=mesh['section'=32,'expert'=8] {'expert'}, dimensions={0} | all-to-all | bytes 327680 | tf_op jit(solution)/shard_map/all_to_all | solution.py:47
  26.1 2.0 gather_fusion.1
  28.3 9.5 %all_to_all.21 = bf16[8,80,128]{2,1,0:T(8,128)(2,1)} all-to-all(bf16[8,80,128]{2,1,0:T(8,128)(2,1)S(1)} %fusion.16), channel_id=1, replica_groups=mesh['section'=32,'expert'=8] {'expert'}, dimensions={0} | all-to-all | bytes 327680 | tf_op jit(solution)/shard_map/all_to_all | solution.py:47
  37.9 77.2 %all-gather.3.cloned.1.call-done = bf16[8,80,4096]{2,1,0:T(8,128)(2,1)} async-done(((bf16[8,80,128]{2,1,0:T(8,128)(2,1)}), bf16[8,80,4096]{2,1,0:T(8,128)(2,1)}) %all-gather.3.cloned.1.call-update) | async-done | bytes 5242896 | tf_op jit(solution)/shard_map/all_gather | solution.py:50
  115.2 5.7 fusion.7
  120.8 2.4 fusion.11
  123.2 81.6 %all-gather.5.cloned.1.call-done = bf16[8,80,4096]{2,1,0:T(8,128)(2,1)} async-done(((bf16[8,80,128]{2,1,0:T(8,128)(2,1)}), bf16[8,80,4096]{2,1,0:T(8,128)(2,1)}) %all-gather.5.cloned.1.call-update) | async-done | bytes 5242896 | tf_op jit(solution)/shard_map/all_gather | solution.py:50
  204.7 5.4 multiply_convert_fusion
  210.1 3.9 convolution_convert_fusion
  214.0 11.2 %copy.36 = bf16[8,80,4096]{1,0,2:T(8,128)(2,1)} copy(bf16[8,80,4096]{2,1,0:T(8,128)(2,1)} %convolution_convert_fusion) | data formatting | bytes 10485760
  225.2 13.1 %reshape.124 = bf16[4096,640]{1,0:T(8,128)(2,1)} reshape(bf16[4096,8,80]{2,1,0:T(8,128)(2,1)} %bitcast.66) | data formatting | bytes 10485760
  238.5 1.3 copy-done.5
  239.8 2.7 fusion.9
  242.5 3.9 add_convert_fusion
  246.4 11.2 %copy.38 = bf16[8,80,4096]{1,0,2:T(8,128)(2,1)} copy(bf16[8,80,4096]{2,1,0:T(8,128)(2,1)} %bitcast.69) | data formatting | bytes 10485760
  257.6 13.1 %reshape.126 = bf16[4096,640]{1,0:T(8,128)(2,1)} reshape(bf16[4096,8,80]{2,1,0:T(8,128)(2,1)} %bitcast.67) | data formatting | bytes 10485760
  271.7 5.7 fusion.1
  277.4 5.8 fusion
  283.2 180.6 %reduce-scatter.7.cloned.1.call-done = bf16[128,640]{1,0:T(8,128)(2,1)} async-done(((bf16[4096,640]{1,0:T(8,128)(2,1)}), bf16[128,640]{1,0:T(8,128)(2,1)}) %reduce-scatter.7.cloned.1.call-update) | async-done | bytes 163856
  463.8 1.2 reshape.125
  465.8 4.8 all-to-all-start.1
  470.6 5.8 fusion.2
  476.4 215.3 %reduce-scatter.9.cloned.1.call-done = bf16[128,640]{1,0:T(8,128)(2,1)} async-done(((bf16[4096,640]{1,0:T(8,128)(2,1)}), bf16[128,640]{1,0:T(8,128)(2,1)}) %reduce-scatter.9.cloned.1.call-update) | async-done | bytes 163856
  691.7 1.2 reshape.127
  693.7 4.8 all-to-all-start.3
  698.5 1.3 gather_fusion.2
  700.3 72.8 %psum.7 = f32[256,2]{0,1:T(2,128)} all-reduce(f32[256,2]{0,1:T(2,128)S(1)} %bitcast.81), channel_id=1, replica_groups=mesh['section'=32,'expert'=8] {'section'}, use_global_device_ids=true, to_apply=%region_11.12 | all-reduce | flops 512 | bytes 4096 | tf_op jit(solution)/shard_map/psum | solution.py:76
  773.2 2.4 fusion.13
  775.6 1.4 fusion.14
  (57 shorter events, 7.0 us)
Async XLA Ops:
  7.2 197.6 %copy-start = (bf16[1,256,4096]{2,1,0:T(8,128)(2,1)S(1)}, bf16[1,256,4096]{2,1,0:T(8,128)(2,1)}, u32[]{:S(2)}) copy-start(bf16[1,256,4096]{2,1,0:T(8,128)(2,1)} %param.12) | copy-start | bytes 6291460
  7.2 6.4 copy-start.2
  7.2 18.9 %copy-start.3 = (bf16[256,128]{1,0:T(8,128)(2,1)S(1)}, bf16[256,128]{1,0:T(8,128)(2,1)}, u32[]{:S(2)}) copy-start(bf16[256,128]{1,0:T(8,128)(2,1)} %param.13) | copy-start | bytes 196612
  7.2 108.0 %all-gather.3.cloned.1.call-start = ((), (), s32[]{:S(2)}) async-start(), calls=%async_computation.6 | async-start | bytes 5406720 | tf_op jit(solution)/shard_map/all_gather | solution.py:50
  26.0 178.7 %all-gather.5.cloned.1.call-start = ((), (), s32[]{:S(2)}) async-start(), calls=%async_computation.7 | async-start | bytes 5406720 | tf_op jit(solution)/shard_map/all_gather | solution.py:50
  37.9 425.9 %reduce-scatter.7.cloned.1.call-start = ((), (), s32[]{:S(2)}) async-start(), calls=%async_computation.8 | async-start | bytes 5406720
  115.2 5.7 copy-start.4
  115.2 5.7 copy-start.10
  238.2 1.6 copy-start.5
  238.3 453.4 %reduce-scatter.9.cloned.1.call-start = ((), (), s32[]{:S(2)}) async-start(), calls=%async_computation.9 | async-start | bytes 5406720
  239.8 2.7 copy-start.6
  239.8 2.7 copy-start.8
  270.7 1.0 copy-start.9
  271.7 5.7 copy-start.7
  465.8 227.9 %all-to-all-start.1 = ((bf16[8,80,128]{2,1,0:T(8,128)(2,1)}), bf16[8,80,128]{2,1,0:T(8,128)(2,1)S(1)}, u32[]{:S(2)}, u32[]{:S(2)}) async-start(bf16[8,80,128]{2,1,0:T(8,128)(2,1)} %copy.37), calls=%async_computation.1 | async-start | bytes 327680 | tf_op jit(solution)/shard_map/all_to_all | solution.py:60
  470.6 306.3 %copy-start.1 = (bf16[1,256,4096]{2,1,0:T(8,128)(2,1)S(1)}, bf16[1,256,4096]{2,1,0:T(8,128)(2,1)}, u32[]{:S(2)}) copy-start(bf16[1,256,4096]{2,1,0:T(8,128)(2,1)} %param.12) | copy-start | bytes 6291460
  693.7 81.9 %all-to-all-start.3 = ((bf16[8,80,128]{2,1,0:T(8,128)(2,1)}), bf16[8,80,128]{2,1,0:T(8,128)(2,1)S(1)}, u32[]{:S(2)}, u32[]{:S(2)}) async-start(bf16[8,80,128]{2,1,0:T(8,128)(2,1)} %copy.39), calls=%async_computation.3 | async-start | bytes 327680 | tf_op jit(solution)/shard_map/all_to_all | solution.py:60
Sparse Core Ops, SparseCore 0:
  26.1 88.9 all-gather.2
  117.6 87.0 all-gather.4
  238.4 225.3 reduce-scatter.6
  467.6 224.0 reduce-scatter.8
where the time goes:
time: 785 us; the launch traced here: 783 us
  waiting for transfers between devices  555 us (71%)
  blocking collectives  92.6 us (12%)
  local copies, waits for them, and re-layouts  62.1 us (8%)
  matrix products  45.3 us (6%)
  between operations  14 us (2%)
  starting transfers between devices  9.93 us (1%)
    unnamed x6, waiting for transfers between devices  396 us
    all_gather x2, waiting for transfers between devices, to_experts(): whole = lax.all_gather(arrived, 'section', axis=2, tiled=True)  159 us
    psum x1, blocking collectives, per_device(): grad_mix = lax.psum(mix_terms, 'section')  72.8 us
    unnamed x31, local copies, waits for them, and re-layouts  55.6 us
    all_to_all x2, blocking collectives, to_experts(): lax.all_to_all(block.reshape(experts, capacity, -1), 'expert', split_axis...  19.8 us
  transfers between devices with their start and end apart: 6, of which 4 were waited for; matrix products, arithmetic and copies ran while one was open for 9% of the time, Pallas kernels for 0%

commit v1 on v0

--- a/solution.py
+++ b/solution.py
@@ -4,6 +4,13 @@
 from jax.sharding import PartitionSpec as P
 
 highest = lax.Precision.HIGHEST
+
+
+def gather_over(block, axis, d):
+    n_dev = lax.axis_size(axis)
+    shards = jnp.stack([block for _ in range(n_dev)])
+    shards = lax.all_to_all(shards, axis, split_axis=0, concat_axis=0)
+    return jnp.concatenate(shards, axis=d)
 
 
 def slot_tables(route_rows, mix_rows, capacity, experts):
@@ -47,7 +54,7 @@
         arrived = lax.all_to_all(
             block.reshape(experts, capacity, -1), "expert", split_axis=0, concat_axis=0, tiled=True
         )
-        whole = lax.all_gather(arrived, "section", axis=2, tiled=True)
+        whole = gather_over(arrived, "section", 2)
         return whole.reshape(slot_total, -1)
 
     def to_sources(partial_value):

time: 785 us -> 885 us (1.13)
  blocking collectives: 92.6 us -> 211 us
  waiting for transfers between devices: 555 us -> 501 us
  local copies, waits for them, and re-layouts: 62.1 us -> 83.7 us
  starting transfers between devices: 9.93 us -> 21 us
    all_gather x2 -> x0, waiting for transfers between devices: 159 us -> none  [to_experts(): whole = lax.all_gather(arrived, 'section', axis=2, tiled=True)]
    all_to_all x0 -> x1, blocking collectives: none -> 129 us  [gather_over(): shards = lax.all_to_all(shards, axis, split_axis=0, concat_axis=0)]
    all_to_all x0 -> x2, waiting for transfers between devices: none -> 113 us  [the longest x1 110 us: gather_over(): shards = lax.all_to_all(shards, axis, split_axis=0, concat_axis=0)]
    reshape x0 -> x2, local copies, waits for them, and re-layouts: none -> 14.3 us  [gather_over(): return jnp.concatenate(shards, axis=d)]
    all_to_all x2 -> x1, blocking collectives: 19.8 us -> 8.86 us  [to_experts(): lax.all_to_all(block.reshape(experts, capacity, -1), 'expert', split_axis...]
    all_to_all x0 -> x2, starting transfers between devices: none -> 10.5 us  [the longest x1 5.48 us: to_experts(): lax.all_to_all(block.reshape(experts, capacity, -1), 'expert', split_axis...]
    unnamed x6 -> x4, waiting for transfers between devices: 396 us -> 388 us
    unnamed x31 -> x45, local copies, waits for them, and re-layouts: 55.6 us -> 57.7 us
  transfers between devices with their start and end apart: 6 -> 6, of which waited for: 4 -> 4; matrix products, arithmetic and copies ran while one was open for 9% -> 8% of each run, Pallas kernels for 0% -> 0%
where the time goes in v1:
time: 885 us; the launch traced here: 878 us
  waiting for transfers between devices  501 us (57%)
  blocking collectives  211 us (24%)
  local copies, waits for them, and re-layouts  83.7 us (9%)
  matrix products  41.7 us (5%)
  starting transfers between devices  21 us (2%)
  between operations  14.7 us (2%)
    unnamed x4, waiting for transfers between devices  388 us
    all_to_all x1, blocking collectives, gather_over(): shards = lax.all_to_all(shards, axis, split_axis=0, concat_axis=0)  129 us
    all_to_all x1, waiting for transfers between devices, gather_over(): shards = lax.all_to_all(shards, axis, split_axis=0, concat_axis=0)  110 us
    psum x1, blocking collectives, per_device(): grad_mix = lax.psum(mix_terms, 'section')  72.9 us
    unnamed x45, local copies, waits for them, and re-layouts  57.7 us
  transfers between devices with their start and end apart: 6, of which 4 were waited for; matrix products, arithmetic and copies ran while one was open for 8% of the time, Pallas kernels for 0%

profile of v1, /device:TPU:8, one launch (start us, length us, event | category | flops | bytes accessed | tf_op | source)
XLA Modules:
  0.0 878.5 jit_solution(14500645729859562221)
XLA Ops:
  11.4 2.3 select_reduce_fusion
  13.8 2.6 gather_fusion
  17.2 5.5 all-to-all-start
  22.7 2.0 gather_fusion.1
  24.9 2.8 all-to-all-done
  27.7 8.9 %all_to_all.30 = bf16[8,80,128]{2,1,0:T(8,128)(2,1)S(1)} all-to-all(bf16[8,80,128]{2,1,0:T(8,128)(2,1)S(1)} %fusion.46), channel_id=1, replica_groups=mesh['section'=32,'expert'=8] {'expert'}, dimensions={0} | all-to-all | bytes 327680 | tf_op jit(solution)/shard_map/all_to_all | solution.py:54
  37.7 129.1 %all_to_all.31 = bf16[32,8,80,128]{3,2,1,0:T(8,128)(2,1)} all-to-all(bf16[32,8,80,128]{3,2,1,0:T(8,128)(2,1)S(1)} %stack.5), channel_id=1, replica_groups=mesh['section'=32,'expert'=8] {'section'}, dimensions={0} | all-to-all | bytes 10485760 | tf_op jit(solution)/shard_map/all_to_all | solution.py:12
  166.8 3.5 stack.4
  170.3 5.1 all-to-all-start.1
  175.9 8.2 copy.38
  184.2 109.8 %all-to-all-done.1 = bf16[32,8,80,128]{3,2,1,0:T(8,128)(2,1)} async-done(((bf16[32,8,80,128]{3,2,1,0:T(8,128)(2,1)}), bf16[32,8,80,128]{3,2,1,0:T(8,128)(2,1)}, u32[]{:S(2)}, u32[]{:S(2)}) %all-to-all-start.1) | async-done | bytes 5242912 | tf_op jit(solution)/shard_map/all_to_all | solution.py:12
  294.0 6.0 copy.37
  300.0 1.7 fusion.8
  303.2 1.7 fusion.10
  305.2 2.4 multiply_convert_fusion
  307.6 3.9 convolution_convert_fusion
  311.5 11.2 %copy.42 = bf16[8,80,4096]{1,0,2:T(8,128)(2,1)} copy(bf16[8,80,4096]{2,1,0:T(8,128)(2,1)} %convolution_convert_fusion) | data formatting | bytes 10485760
  322.6 13.1 %reshape.128 = bf16[4096,640]{1,0:T(8,128)(2,1)} reshape(bf16[4096,8,80]{2,1,0:T(8,128)(2,1)} %bitcast.92) | data formatting | bytes 10485760
  335.8 1.5 copy-done.7
  337.3 1.6 fusion.40
  338.9 4.0 add_convert_fusion
  342.9 11.2 %copy.44 = bf16[8,80,4096]{1,0,2:T(8,128)(2,1)} copy(bf16[8,80,4096]{2,1,0:T(8,128)(2,1)} %bitcast.100) | data formatting | bytes 10485760
  354.1 13.3 %reshape.130 = bf16[4096,640]{1,0:T(8,128)(2,1)} reshape(bf16[4096,8,80]{2,1,0:T(8,128)(2,1)} %bitcast.93) | data formatting | bytes 10485760
  368.4 9.5 %fusion.24 = bf16[1,4096,256]{2,1,0:T(8,128)(2,1)} fusion(bf16[640,256]{1,0:T(8,128)(2,1)S(1)} %copy-done.13, bf16[80,8,32,128]{3,2,1,0:T(8,128)(2,1)} %bitcast.105), kind=kOutput, calls=%fused_computation.21 | convolution fusion | flops 1343225856 | bytes 7667712 | tf_op jit(solution)/shard_map/dot_general | solution.py:97
  377.8 6.8 fusion.27
  384.6 173.9 %reduce-scatter.7.cloned.1.call-done = bf16[128,640]{1,0:T(8,128)(2,1)} async-done(((bf16[4096,640]{1,0:T(8,128)(2,1)}), bf16[128,640]{1,0:T(8,128)(2,1)}) %reduce-scatter.7.cloned.1.call-update) | async-done | bytes 163856
  560.5 5.1 all-to-all-start.2
  565.6 6.1 fusion.21
  571.7 214.4 %reduce-scatter.9.cloned.1.call-done = bf16[128,640]{1,0:T(8,128)(2,1)} async-done(((bf16[4096,640]{1,0:T(8,128)(2,1)}), bf16[128,640]{1,0:T(8,128)(2,1)}) %reduce-scatter.9.cloned.1.call-update) | async-done | bytes 163856
  788.1 4.8 all-to-all-start.5
  794.7 72.9 %psum.7 = f32[256,2]{0,1:T(2,128)} all-reduce(f32[256,2]{0,1:T(2,128)S(1)} %bitcast.116), channel_id=1, replica_groups=mesh['section'=32,'expert'=8] {'section'}, use_global_device_ids=true, to_apply=%region_11.12 | all-reduce | flops 512 | bytes 4096 | tf_op jit(solution)/shard_map/psum | solution.py:83
  867.6 2.4 fusion.43
  (75 shorter events, 17.0 us)
Async XLA Ops:
  7.2 297.7 %copy-start = (bf16[1,256,4096]{2,1,0:T(8,128)(2,1)S(1)}, bf16[1,256,4096]{2,1,0:T(8,128)(2,1)}, u32[]{:S(2)}) copy-start(bf16[1,256,4096]{2,1,0:T(8,128)(2,1)} %param.12) | copy-start | bytes 6291460
  7.2 15.5 %copy-start.3 = (bf16[256,128]{1,0:T(8,128)(2,1)S(1)}, bf16[256,128]{1,0:T(8,128)(2,1)}, u32[]{:S(2)}) copy-start(bf16[256,128]{1,0:T(8,128)(2,1)} %param.13) | copy-start | bytes 196612
  17.2 10.5 %all-to-all-start = ((bf16[8,80,128]{2,1,0:T(8,128)(2,1)}), bf16[8,80,128]{2,1,0:T(8,128)(2,1)S(1)}, u32[]{:S(2)}, u32[]{:S(2)}) async-start(bf16[8,80,128]{2,1,0:T(8,128)(2,1)} %fusion.47), calls=%async_computation | async-start | bytes 327680 | tf_op jit(solution)/shard_map/all_to_all | solution.py:54
  170.3 123.7 %all-to-all-start.1 = ((bf16[32,8,80,128]{3,2,1,0:T(8,128)(2,1)}), bf16[32,8,80,128]{3,2,1,0:T(8,128)(2,1)}, u32[]{:S(2)}, u32[]{:S(2)}) async-start(bf16[32,8,80,128]{3,2,1,0:T(8,128)(2,1)} %stack.4), calls=%async_computation.1 | async-start | bytes 10485760 | tf_op jit(solution)/shard_map/all_to_all | solution.py:12
  175.3 383.1 %reduce-scatter.7.cloned.1.call-start = ((), (), s32[]{:S(2)}) async-start(), calls=%async_computation.8 | async-start | bytes 5406720
  294.0 6.0 copy-start.8
  300.0 2.8 copy-start.4
  300.0 3.2 copy-start.6
  300.0 4.9 slice-start
  303.2 2.0 slice-start.1
  307.6 28.2 %copy-start.10 = (bf16[640,256]{1,0:T(8,128)(2,1)}, bf16[640,256]{1,0:T(8,128)(2,1)S(1)}, u32[]{:S(2)}) copy-start(bf16[640,256]{1,0:T(8,128)(2,1)S(1)} %get-tuple-element.13) | copy-start | bytes 983044
  307.6 31.3 %copy-start.12 = (bf16[640,256]{1,0:T(8,128)(2,1)}, bf16[640,256]{1,0:T(8,128)(2,1)S(1)}, u32[]{:S(2)}) copy-start(bf16[640,256]{1,0:T(8,128)(2,1)S(1)} %get-tuple-element.12) | copy-start | bytes 983044
  335.7 1.6 copy-start.7
  335.8 450.3 %reduce-scatter.9.cloned.1.call-start = ((), (), s32[]{:S(2)}) async-start(), calls=%async_computation.9 | async-start | bytes 5406720
  337.3 1.6 copy-start.9
  367.4 1.0 copy-start.13
  367.4 10.4 %slice-start.2 = ((s8[5242880]{0:T(1024)(128)(4,1)}), s8[1048576]{0:T(1024)(128)(4,1)S(1)}, s32[]{:S(2)}) async-start(s8[5242880]{0:T(1024)(128)(4,1)} %bitcast.106), calls=%async_computation.12 | async-start | bytes 2097152
  368.4 9.5 %slice-start.3 = ((s8[5242880]{0:T(1024)(128)(4,1)}), s8[4194304]{0:T(1024)(128)(4,1)S(1)}, s32[]{:S(2)}) async-start(s8[5242880]{0:T(1024)(128)(4,1)} %bitcast.106), calls=%async_computation.13 | async-start | bytes 8388608
  368.4 9.5 %copy-start.11 = (bf16[640,256]{1,0:T(8,128)(2,1)S(1)}, bf16[640,256]{1,0:T(8,128)(2,1)}, u32[]{:S(2)}) copy-start(bf16[640,256]{1,0:T(8,128)(2,1)} %copy-done.10) | copy-start | bytes 983044
  560.5 227.6 %all-to-all-start.2 = ((bf16[8,80,128]{2,1,0:T(8,128)(2,1)}), bf16[8,80,128]{2,1,0:T(8,128)(2,1)S(1)}, u32[]{:S(2)}, u32[]{:S(2)}) async-start(bf16[8,80,128]{2,1,0:T(8,128)(2,1)} %copy.43), calls=%async_computation.2 | async-start | bytes 327680 | tf_op jit(solution)/shard_map/all_to_all | solution.py:67
  565.6 302.0 %copy-start.2 = (bf16[256,128]{1,0:T(8,128)(2,1)S(1)}, bf16[256,128]{1,0:T(8,128)(2,1)}, u32[]{:S(2)}) copy-start(bf16[256,128]{1,0:T(8,128)(2,1)} %param.7) | copy-start | bytes 196612
  565.6 304.4 %copy-start.5 = (f32[640,256]{1,0:T(8,128)S(1)}, f32[640,256]{1,0:T(8,128)}, u32[]{:S(2)}) copy-start(f32[640,256]{1,0:T(8,128)} %get-tuple-element.9) | copy-start | bytes 1966084
  565.6 305.8 %copy-start.1 = (bf16[1,256,4096]{2,1,0:T(8,128)(2,1)S(1)}, bf16[1,256,4096]{2,1,0:T(8,128)(2,1)}, u32[]{:S(2)}) copy-start(bf16[1,256,4096]{2,1,0:T(8,128)(2,1)} %param.12) | copy-start | bytes 6291460
  788.1 81.9 %all-to-all-start.5 = ((bf16[8,80,128]{2,1,0:T(8,128)(2,1)}), bf16[8,80,128]{2,1,0:T(8,128)(2,1)S(1)}, u32[]{:S(2)}, u32[]{:S(2)}) async-start(bf16[8,80,128]{2,1,0:T(8,128)(2,1)} %copy.45), calls=%async_computation.5 | async-start | bytes 327680 | tf_op jit(solution)/shard_map/all_to_all | solution.py:67
Sparse Core Ops, SparseCore 0:
  335.9 222.5 reduce-scatter.6
  562.4 223.6 reduce-scatter.8
